TPU v7x, 32 devices: a whole 2x2x4 slice. The times are simulated.
32 devices in a mesh: groups: 2 (over y), blk: 4 (over z), head: 2 (over x), rep: 2 (over core).
Axes of the slice: x: 2, y: 2, z: 4, core: 2. Of those that a mesh axis runs over, the one named last changes fastest.
Arguments:
- query: bfloat16 [128, 16384], P(('groups', 'blk', 'rep'), 'head'), parts along dimension 0, may hold values from -200 to 200
- keys: bfloat16 [8, 2, 2048, 8, 128], P(('groups', 'blk'), 'rep', None, 'head'), parts along dimension 0, may hold values from -8 to 8
- values: bfloat16 [8, 2, 2048, 8, 128], P(('groups', 'blk'), 'rep', None, 'head'), parts along dimension 0, may hold values from -6 to 6
- lengths: int32 [128], P('groups'), parts along dimension 0, may hold values from 2 to 8192, as said below
- out_weight: bfloat16 [16384, 16384], P('head', ('blk', 'rep')), may hold values from -0.046875 to 0.046875
Outputs:
- projected: bfloat16 [128, 16384], P(('groups', 'head'), ('blk', 'rep')), parts along dimension 0
There are 2 independent parts, one for each index of `groups`. A program takes and returns all parts, laid end to end along the dimension named above; an argument that names none is the same for every part. Nothing has to cross between parts.
Inputs may be any that keep to these rules, and one draw needn't show every extreme that they name: `lengths`: some request of every draw sees all 8192 positions.
All inputs are finite; a program needn't handle non-finite values.
Results may differ from a plain program's by a relative error of at most 0.012.
Values may be sent and summed in bfloat16 or wider, within the bound.
A program may use at most 128 MiB of HBM per device.

v0:
```python
import jax
import jax.numpy as jnp
from jax import lax
from jax.sharding import PartitionSpec as P

NEG = -1e30


def shifted(x, axis, by):
    devices = lax.axis_size(axis)
    return lax.ppermute(x, axis, [(i, (i + by) % devices) for i in range(devices)])


def stop_partial(visiting, row_lengths, positions, key_slot, value_slot, score_scale):
    row_count = visiting.shape[0]
    kv_heads = key_slot.shape[1]
    head_dim = key_slot.shape[2]
    queries = visiting.reshape(row_count, kv_heads, -1, head_dim)
    scores = (
        jnp.einsum("rkgd,jkd->rkgj", queries, key_slot, preferred_element_type=jnp.float32)
        * score_scale
    )
    live_mask = (positions[None, :] < row_lengths[:, None])[:, None, None, :]
    best_score = jnp.max(jnp.where(live_mask, scores, NEG), axis=-1)
    weights = jnp.where(live_mask, jnp.exp(scores - best_score[..., None]), 0.0)
    block_sum = jnp.sum(weights, axis=-1)
    partial_value = jnp.einsum(
        "rkgj,jkd->rkgd",
        weights.astype(jnp.bfloat16),
        value_slot,
        preferred_element_type=jnp.float32,
    )
    return (partial_value.astype(jnp.bfloat16), best_score, block_sum)


def body(query, keys, values, lengths, out_weight):
    row_count = query.shape[0]
    slab_len = keys.shape[2]
    head_dim = keys.shape[4]
    score_scale = head_dim ** (-0.5)
    blocks = lax.axis_size("blk")
    replicas = lax.axis_size("rep")
    span_count = min(8, blocks)
    stride = blocks // span_count
    holder = lax.axis_index("blk")
    rep_index = lax.axis_index("rep")
    key_slot = keys[0, 0]
    value_slot = values[0, 0]
    positions = holder // stride * slab_len + jnp.arange(slab_len, dtype=jnp.int32)
    visiting = query
    stored = []
    for stop_index in range(span_count):
        if stop_index > 0:
            visiting = shifted(visiting, "blk", stride)
        owner_index = (holder - stop_index * stride) % blocks
        first_row = (owner_index * replicas + rep_index) * row_count
        row_lengths = lax.dynamic_slice_in_dim(lengths, first_row, row_count, 0)
        stop_piece = stop_partial(
            visiting, row_lengths, positions, key_slot, value_slot, score_scale
        )
        stored.append(stop_piece)
    outs_home = [stored[0][0]]
    best_home = [stored[0][1]]
    sums_home = [stored[0][2]]
    for stop_index in range(1, span_count):
        outs_home.append(shifted(stored[stop_index][0], "blk", -stop_index * stride))
        stats_home = shifted(
            (stored[stop_index][1], stored[stop_index][2]), "blk", -stop_index * stride
        )
        best_home.append(stats_home[0])
        sums_home.append(stats_home[1])
    best_all = jnp.stack(best_home)
    overall = jnp.max(best_all, axis=0)
    factors = jnp.exp(best_all - overall[None])
    total_sum = jnp.sum(factors * jnp.stack(sums_home), axis=0)
    total_out = jnp.sum(factors[..., None] * jnp.stack(outs_home).astype(jnp.float32), axis=0)
    attended = (total_out / total_sum[..., None]).astype(jnp.bfloat16).reshape(row_count, -1)
    gathered = lax.all_gather(attended, ("blk", "rep"), axis=0, tiled=True)
    projected = lax.psum_scatter(
        jnp.dot(gathered, out_weight, preferred_element_type=jnp.float32),
        "head",
        scatter_dimension=0,
        tiled=True,
    )
    return projected.astype(jnp.bfloat16)


def solution(mesh):
    return jax.shard_map(
        body,
        mesh=mesh,
        in_specs=(
            P(("groups", "blk", "rep"), "head"),
            P(("groups", "blk"), "rep", None, "head", None),
            P(("groups", "blk"), "rep", None, "head", None),
            P("groups"),
            P("head", ("blk", "rep")),
        ),
        out_specs=P(("groups", "head"), ("blk", "rep")),
        check_vma=False,
    )
```

profile of v0, /device:TPU:0, one launch (start us, length us, event | category | flops | bytes accessed | tf_op | source)
XLA Modules:
  0.0 113.8 jit_solution(224056178729096985)
XLA Ops:
  6.5 3.1 %collective-permute-start = (bf16[8,8192]{1,0:T(8,128)(2,1)}, bf16[8,8192]{1,0:T(8,128)(2,1)S(1)}, u32[]{:S(2)}, u32[]{:S(2)}) collective-permute-start(bf16[8,8192]{1,0:T(8,128)(2,1)} %param.5), channel_id=1, source_target_pairs={{0,4},{4,8},{8,12},{12,0},{1,5},{5,9},{9,13},{13,1},{2,6},{6,10},{... | collective-permute-start | bytes 393224 | tf_op jit(solution)/shard_map/ppermute | solution.py:11
  9.6 0.9 fusion.111
  10.5 0.1 broadcast_compare_fusion.3
  10.6 2.7 %fusion.9 = (f32[8,4,16]{2,0,1:T(8,128)S(1)}, f32[4,2048,8,16]{1,3,2,0:T(8,128)S(1)}) fusion(pred[8,2048]{1,0:T(8,128)(4,1)S(1)} %get-tuple-element.7, bf16[8,4,16,128]{3,0,2,1:T(8,128)(2,1)} %bitcast.149, bf16[2048,4,128,1]{2,1,0,3:T(4,128)(2,1)} %bitcast.145), kind=kOutput, calls=%fused_computation.17 | convolution fusion | flops 271580672 | bytes 6440960 | tf_op jit(solution)/shard_map/rkgd,jkd->rkgj/dot_general | solution.py:20
  13.3 1.2 %fusion.91 = bf16[1,8,4,16,128]{4,3,1,2,0:T(8,128)(2,1)S(1)} fusion(bf16[2048,4,128,1]{2,1,0,3:T(4,128)(2,1)S(1)} %bitcast.122, f32[4,2048,8,16]{1,3,2,0:T(8,128)S(1)} %get-tuple-element.22, f32[8,4,16]{2,0,1:T(8,128)S(1)} %get-tuple-element.21, pred[8,2048]{1,0:T(8,128)(4,1)S(1)} %get-tuple-element.7), kind=kOutput, calls=%fused_computation.67 | convolution fusion | flops 272695296 | bytes 6440960 | tf_op jit(solution)/shard_map/rkgj,jkd->rkgd/dot_general | solution.py:27
  14.5 0.0 copy-start.1
  14.6 1.1 fusion.12
  15.7 0.0 collective-permute-done
  15.7 0.4 copy-done.1
  16.1 1.1 fusion.6
  17.3 1.2 %fusion.86 = bf16[8,4,16,128]{3,2,0,1:T(8,128)(2,1)S(1)} fusion(bf16[2048,4,128,1]{2,1,0,3:T(4,128)(2,1)S(1)} %bitcast.125, f32[4,2048,8,16]{1,3,2,0:T(8,128)S(1)} %get-tuple-element.20, f32[8,4,16]{2,0,1:T(8,128)S(1)} %get-tuple-element.19, pred[8,2048]{1,0:T(8,128)(4,1)S(1)} %get-tuple-element.8), kind=kOutput, calls=%fused_computation.66 | convolution fusion | flops 272695296 | bytes 6440960 | tf_op jit(solution)/shard_map/rkgj,jkd->rkgd/dot_general | solution.py:27
  18.5 1.6 %collective-permute-start.2 = (bf16[8,8192]{1,0:T(8,128)(2,1)S(1)}, bf16[8,8192]{1,0:T(8,128)(2,1)S(1)}, u32[]{:S(2)}, u32[]{:S(2)}) collective-permute-start(bf16[8,8192]{1,0:T(8,128)(2,1)S(1)} %collective-permute-done), channel_id=1, source_target_pairs={{0,4},{4,8},{8,12},{12,0},{1,5},{5,9},{9,13},{13,1},{2,6},{6,10},{... | collective-permute-start | bytes 393224 | tf_op jit(solution)/shard_map/ppermute | solution.py:11
  20.1 1.1 fusion.14
  21.2 2.3 %collective-permute-start.1 = (f32[8,4,16]{2,0,1:T(8,128)S(1)}, f32[8,4,16]{2,0,1:T(8,128)S(1)}, u32[]{:S(2)}, u32[]{:S(2)}) collective-permute-start(f32[8,4,16]{2,0,1:T(8,128)S(1)} %get-tuple-element.19), channel_id=1, source_target_pairs={{0,12},{4,0},{8,4},{12,8},{1,13},{5,1},{9,5},{13,9},{2,14},{6,2},{... | collective-permute-start | bytes 6152 | tf_op jit(solution)/shard_map/ppermute | solution.py:11
  23.5 0.3 collective-permute-start.9
  23.8 2.0 %collective-permute-start.6 = (bf16[8,4,16,128]{3,2,0,1:T(8,128)(2,1)S(1)}, bf16[8,4,16,128]{3,2,0,1:T(8,128)(2,1)S(1)}, u32[]{:S(2)}, u32[]{:S(2)}) collective-permute-start(bf16[8,4,16,128]{3,2,0,1:T(8,128)(2,1)S(1)} %fusion.86), channel_id=1, source_target_pairs={{0,12},{4,0},{8,4},{12,8},{1,13},{5,1},{9,5},{13,9},{2,14},{6,2},{... | collective-permute-start | bytes 393224 | tf_op jit(solution)/shard_map/ppermute | solution.py:11
  25.8 0.0 collective-permute-done.2
  25.8 1.1 fusion.3
  26.9 1.2 %fusion.81 = bf16[8,4,16,128]{3,2,0,1:T(8,128)(2,1)S(1)} fusion(bf16[2048,4,128,1]{2,1,0,3:T(4,128)(2,1)S(1)} %bitcast.124, f32[4,2048,8,16]{1,3,2,0:T(8,128)S(1)} %get-tuple-element.18, f32[8,4,16]{2,0,1:T(8,128)S(1)} %get-tuple-element.17, pred[8,2048]{1,0:T(8,128)(4,1)S(1)} %get-tuple-element.9), kind=kOutput, calls=%fused_computation.65 | convolution fusion | flops 272695296 | bytes 6440960 | tf_op jit(solution)/shard_map/rkgj,jkd->rkgd/dot_general | solution.py:27
  28.2 0.3 collective-permute-start.4
  28.4 1.1 fusion.16
  29.5 1.2 %collective-permute-start.3 = (f32[8,4,16]{2,0,1:T(8,128)S(1)}, f32[8,4,16]{2,0,1:T(8,128)S(1)}, u32[]{:S(2)}, u32[]{:S(2)}) collective-permute-start(f32[8,4,16]{2,0,1:T(8,128)S(1)} %get-tuple-element.17), channel_id=1, source_target_pairs={{0,8},{4,12},{8,0},{12,4},{1,9},{5,13},{9,1},{13,5},{2,10},{6,14},... | collective-permute-start | bytes 6152 | tf_op jit(solution)/shard_map/ppermute | solution.py:11
  30.8 4.5 %collective-permute-done.4 = bf16[8,8192]{1,0:T(8,128)(2,1)S(1)} collective-permute-done((bf16[8,8192]{1,0:T(8,128)(2,1)S(1)}, bf16[8,8192]{1,0:T(8,128)(2,1)S(1)}, u32[]{:S(2)}, u32[]{:S(2)}) %collective-permute-start.4) | collective-permute-done | bytes 131104 | tf_op jit(solution)/shard_map/ppermute | solution.py:11
  35.3 1.1 fusion
  36.4 0.1 collective-permute-start.5
  36.5 1.2 %fusion.76 = bf16[8,4,16,128]{3,2,0,1:T(8,128)(2,1)S(1)} fusion(bf16[2048,4,128,1]{2,1,0,3:T(4,128)(2,1)S(1)} %bitcast.123, f32[4,2048,8,16]{1,3,2,0:T(8,128)S(1)} %get-tuple-element.16, f32[8,4,16]{2,0,1:T(8,128)S(1)} %get-tuple-element.15, pred[8,2048]{1,0:T(8,128)(4,1)S(1)} %get-tuple-element.10), kind=kOutput, calls=%fused_computation.64 | convolution fusion | flops 272695296 | bytes 6440960 | tf_op jit(solution)/shard_map/rkgj,jkd->rkgd/dot_general | solution.py:27
  37.7 1.1 fusion.18
  38.8 0.0 collective-permute-done.1
  38.8 0.2 collective-permute-start.10
  39.0 2.8 %collective-permute-start.7 = (bf16[8,4,16,128]{3,2,0,1:T(8,128)(2,1)S(1)}, bf16[8,4,16,128]{3,2,0,1:T(8,128)(2,1)S(1)}, u32[]{:S(2)}, u32[]{:S(2)}) collective-permute-start(bf16[8,4,16,128]{3,2,0,1:T(8,128)(2,1)S(1)} %fusion.81), channel_id=1, source_target_pairs={{0,8},{4,12},{8,0},{12,4},{1,9},{5,13},{9,1},{13,5},{2,10},{6,14},... | collective-permute-start | bytes 393224 | tf_op jit(solution)/shard_map/ppermute | solution.py:11
  41.8 0.3 collective-permute-done.5
  42.1 1.2 %collective-permute-start.11 = (f32[8,4,16]{2,0,1:T(8,128)S(1)}, f32[8,4,16]{2,0,1:T(8,128)S(1)}, u32[]{:S(2)}, u32[]{:S(2)}) collective-permute-start(f32[8,4,16]{2,0,1:T(8,128)S(1)} %fusion.18), channel_id=1, source_target_pairs={{0,4},{4,8},{8,12},{12,0},{1,5},{5,9},{9,13},{13,1},{2,6},{6,10},{... | collective-permute-start | bytes 6152 | tf_op jit(solution)/shard_map/ppermute | solution.py:11
  43.3 0.1 collective-permute-start.8
  43.4 2.8 %collective-permute-done.10 = f32[8,4,16]{2,0,1:T(8,128)S(1)} collective-permute-done((f32[8,4,16]{2,0,1:T(8,128)S(1)}, f32[8,4,16]{2,0,1:T(8,128)S(1)}, u32[]{:S(2)}, u32[]{:S(2)}) %collective-permute-start.10) | collective-permute-done | bytes 2080 | tf_op jit(solution)/shard_map/ppermute | solution.py:11
  46.2 2.6 %collective-permute-done.11 = f32[8,4,16]{2,0,1:T(8,128)S(1)} collective-permute-done((f32[8,4,16]{2,0,1:T(8,128)S(1)}, f32[8,4,16]{2,0,1:T(8,128)S(1)}, u32[]{:S(2)}, u32[]{:S(2)}) %collective-permute-start.11) | collective-permute-done | bytes 2080 | tf_op jit(solution)/shard_map/ppermute | solution.py:11
  48.8 0.0 collective-permute-done.6
  48.9 1.7 %collective-permute-done.7 = bf16[8,4,16,128]{3,2,0,1:T(8,128)(2,1)S(1)} collective-permute-done((bf16[8,4,16,128]{3,2,0,1:T(8,128)(2,1)S(1)}, bf16[8,4,16,128]{3,2,0,1:T(8,128)(2,1)S(1)}, u32[]{:S(2)}, u32[]{:S(2)}) %collective-permute-start.7) | collective-permute-done | bytes 131104 | tf_op jit(solution)/shard_map/ppermute | solution.py:11
  50.6 0.0 collective-permute-done.8
  50.6 0.3 multiply_reduce_fusion
  50.9 0.1 divide_convert_fusion
  51.1 0.7 copy.137
  51.9 0.0 all-gather.2.cloned.1.call-update
  51.9 0.0 reduce-scatter.2.cloned.1.call-start
  51.9 21.4 %all-gather.2.cloned.1.call-done = bf16[64,8192]{1,0:T(8,128)(2,1)} async-done(((bf16[8,8192]{1,0:T(8,128)(2,1)}), bf16[64,8192]{1,0:T(8,128)(2,1)}) %all-gather.2.cloned.1.call-update) | async-done | bytes 1048592 | tf_op jit(solution)/shard_map/all_gather | solution.py:78
  73.3 17.6 %fusion.112 = f32[64,2048]{1,0:T(8,128)} fusion(bf16[64,8192]{1,0:T(8,128)(2,1)} %all-gather.2.cloned.1.call-done, bf16[8192,2048]{1,0:T(8,128)(2,1)} %param.9), kind=kOutput, calls=%fused_computation.94 | convolution fusion | flops 2147483648 | bytes 35127296 | tf_op jit(solution)/shard_map/dot_general | solution.py:80
  91.0 0.0 reduce-scatter.2.cloned.1.call-update
  91.0 14.4 %reduce-scatter.2.cloned.1.call-done = f32[32,2048]{1,0:T(8,128)} async-done(((f32[64,2048]{1,0:T(8,128)}), f32[32,2048]{1,0:T(8,128)}) %reduce-scatter.2.cloned.1.call-update) | async-done | bytes 262160 | tf_op jit(solution)/shard_map/reduce_scatter | solution.py:79
  105.4 1.6 %convert_element_type.64 = bf16[32,2048]{1,0:T(8,128)(2,1)} convert(f32[32,2048]{1,0:T(8,128)} %reduce-scatter.2.cloned.1.call-done) | non-fusion elementwise | flops 65536 | bytes 393216 | tf_op jit(solution)/shard_map/convert_element_type | solution.py:85
  (12 shorter events, 0.1 us)
Async XLA Ops:
  6.5 6.8 %copy-start = (bf16[1,1,2048,4,128]{4,3,2,1,0:T(4,128)(2,1)S(1)}, bf16[1,1,2048,4,128]{4,3,2,1,0:T(4,128)(2,1)}, u32[]{:S(2)}) copy-start(bf16[1,1,2048,4,128]{4,3,2,1,0:T(4,128)(2,1)} %param.7) | copy-start | bytes 6291460
  6.5 66.8 %all-gather.2.cloned.1.call-start = ((), (), s32[]{:S(2)}) async-start(), calls=%async_computation.1 | async-start | bytes 1179648 | tf_op jit(solution)/shard_map/all_gather | solution.py:78
  6.5 9.1 %collective-permute-start = (bf16[8,8192]{1,0:T(8,128)(2,1)}, bf16[8,8192]{1,0:T(8,128)(2,1)S(1)}, u32[]{:S(2)}, u32[]{:S(2)}) collective-permute-start(bf16[8,8192]{1,0:T(8,128)(2,1)} %param.5), channel_id=1, source_target_pairs={{0,4},{4,8},{8,12},{12,0},{1,5},{5,9},{9,13},{13,1},{2,6},{6,10},{... | collective-permute-start | bytes 393224 | tf_op jit(solution)/shard_map/ppermute | solution.py:11
  14.5 1.6 %copy-start.1 = (bf16[1,1,2048,4,128]{4,3,2,1,0:T(4,128)(2,1)S(1)}, bf16[1,1,2048,4,128]{4,3,2,1,0:T(4,128)(2,1)}, u32[]{:S(2)}) copy-start(bf16[1,1,2048,4,128]{4,3,2,1,0:T(4,128)(2,1)} %param.6) | copy-start | bytes 6291460
  18.5 7.3 %collective-permute-start.2 = (bf16[8,8192]{1,0:T(8,128)(2,1)S(1)}, bf16[8,8192]{1,0:T(8,128)(2,1)S(1)}, u32[]{:S(2)}, u32[]{:S(2)}) collective-permute-start(bf16[8,8192]{1,0:T(8,128)(2,1)S(1)} %collective-permute-done), channel_id=1, source_target_pairs={{0,4},{4,8},{8,12},{12,0},{1,5},{5,9},{9,13},{13,1},{2,6},{6,10},{... | collective-permute-start | bytes 393224 | tf_op jit(solution)/shard_map/ppermute | solution.py:11
  21.2 17.6 %collective-permute-start.1 = (f32[8,4,16]{2,0,1:T(8,128)S(1)}, f32[8,4,16]{2,0,1:T(8,128)S(1)}, u32[]{:S(2)}, u32[]{:S(2)}) collective-permute-start(f32[8,4,16]{2,0,1:T(8,128)S(1)} %get-tuple-element.19), channel_id=1, source_target_pairs={{0,12},{4,0},{8,4},{12,8},{1,13},{5,1},{9,5},{13,9},{2,14},{6,2},{... | collective-permute-start | bytes 6152 | tf_op jit(solution)/shard_map/ppermute | solution.py:11
  23.5 19.8 %collective-permute-start.9 = (f32[8,4,16]{2,0,1:T(8,128)S(1)}, f32[8,4,16]{2,0,1:T(8,128)S(1)}, u32[]{:S(2)}, u32[]{:S(2)}) collective-permute-start(f32[8,4,16]{2,0,1:T(8,128)S(1)} %fusion.14), channel_id=1, source_target_pairs={{0,12},{4,0},{8,4},{12,8},{1,13},{5,1},{9,5},{13,9},{2,14},{6,2},{... | collective-permute-start | bytes 6152 | tf_op jit(solution)/shard_map/ppermute | solution.py:11
  23.8 25.0 %collective-permute-start.6 = (bf16[8,4,16,128]{3,2,0,1:T(8,128)(2,1)S(1)}, bf16[8,4,16,128]{3,2,0,1:T(8,128)(2,1)S(1)}, u32[]{:S(2)}, u32[]{:S(2)}) collective-permute-start(bf16[8,4,16,128]{3,2,0,1:T(8,128)(2,1)S(1)} %fusion.86), channel_id=1, source_target_pairs={{0,12},{4,0},{8,4},{12,8},{1,13},{5,1},{9,5},{13,9},{2,14},{6,2},{... | collective-permute-start | bytes 393224 | tf_op jit(solution)/shard_map/ppermute | solution.py:11
  28.2 7.1 %collective-permute-start.4 = (bf16[8,8192]{1,0:T(8,128)(2,1)S(1)}, bf16[8,8192]{1,0:T(8,128)(2,1)S(1)}, u32[]{:S(2)}, u32[]{:S(2)}) collective-permute-start(bf16[8,8192]{1,0:T(8,128)(2,1)S(1)} %collective-permute-done.2), channel_id=1, source_target_pairs={{0,4},{4,8},{8,12},{12,0},{1,5},{5,9},{9,13},{13,1},{2,6},{6,10},{... | collective-permute-start | bytes 393224 | tf_op jit(solution)/shard_map/ppermute | solution.py:11
  29.5 9.4 %collective-permute-start.3 = (f32[8,4,16]{2,0,1:T(8,128)S(1)}, f32[8,4,16]{2,0,1:T(8,128)S(1)}, u32[]{:S(2)}, u32[]{:S(2)}) collective-permute-start(f32[8,4,16]{2,0,1:T(8,128)S(1)} %get-tuple-element.17), channel_id=1, source_target_pairs={{0,8},{4,12},{8,0},{12,4},{1,9},{5,13},{9,1},{13,5},{2,10},{6,14},... | collective-permute-start | bytes 6152 | tf_op jit(solution)/shard_map/ppermute | solution.py:11
  36.4 5.7 %collective-permute-start.5 = (f32[8,4,16]{2,0,1:T(8,128)S(1)}, f32[8,4,16]{2,0,1:T(8,128)S(1)}, u32[]{:S(2)}, u32[]{:S(2)}) collective-permute-start(f32[8,4,16]{2,0,1:T(8,128)S(1)} %get-tuple-element.15), channel_id=1, source_target_pairs={{0,4},{4,8},{8,12},{12,0},{1,5},{5,9},{9,13},{13,1},{2,6},{6,10},{... | collective-permute-start | bytes 6152 | tf_op jit(solution)/shard_map/ppermute | solution.py:11
  38.8 7.4 %collective-permute-start.10 = (f32[8,4,16]{2,0,1:T(8,128)S(1)}, f32[8,4,16]{2,0,1:T(8,128)S(1)}, u32[]{:S(2)}, u32[]{:S(2)}) collective-permute-start(f32[8,4,16]{2,0,1:T(8,128)S(1)} %fusion.16), channel_id=1, source_target_pairs={{0,8},{4,12},{8,0},{12,4},{1,9},{5,13},{9,1},{13,5},{2,10},{6,14},... | collective-permute-start | bytes 6152 | tf_op jit(solution)/shard_map/ppermute | solution.py:11
  39.0 11.6 %collective-permute-start.7 = (bf16[8,4,16,128]{3,2,0,1:T(8,128)(2,1)S(1)}, bf16[8,4,16,128]{3,2,0,1:T(8,128)(2,1)S(1)}, u32[]{:S(2)}, u32[]{:S(2)}) collective-permute-start(bf16[8,4,16,128]{3,2,0,1:T(8,128)(2,1)S(1)} %fusion.81), channel_id=1, source_target_pairs={{0,8},{4,12},{8,0},{12,4},{1,9},{5,13},{9,1},{13,5},{2,10},{6,14},... | collective-permute-start | bytes 393224 | tf_op jit(solution)/shard_map/ppermute | solution.py:11
  42.1 6.7 %collective-permute-start.11 = (f32[8,4,16]{2,0,1:T(8,128)S(1)}, f32[8,4,16]{2,0,1:T(8,128)S(1)}, u32[]{:S(2)}, u32[]{:S(2)}) collective-permute-start(f32[8,4,16]{2,0,1:T(8,128)S(1)} %fusion.18), channel_id=1, source_target_pairs={{0,4},{4,8},{8,12},{12,0},{1,5},{5,9},{9,13},{13,1},{2,6},{6,10},{... | collective-permute-start | bytes 6152 | tf_op jit(solution)/shard_map/ppermute | solution.py:11
  43.3 7.3 %collective-permute-start.8 = (bf16[8,4,16,128]{3,2,0,1:T(8,128)(2,1)S(1)}, bf16[8,4,16,128]{3,2,0,1:T(8,128)(2,1)S(1)}, u32[]{:S(2)}, u32[]{:S(2)}) collective-permute-start(bf16[8,4,16,128]{3,2,0,1:T(8,128)(2,1)S(1)} %fusion.76), channel_id=1, source_target_pairs={{0,4},{4,8},{8,12},{12,0},{1,5},{5,9},{9,13},{13,1},{2,6},{6,10},{... | collective-permute-start | bytes 393224 | tf_op jit(solution)/shard_map/ppermute | solution.py:11
  51.9 53.5 %reduce-scatter.2.cloned.1.call-start = ((), (), s32[]{:S(2)}) async-start(), calls=%async_computation.2 | async-start | bytes 786432 | tf_op jit(solution)/shard_map/reduce_scatter | solution.py:79
Sparse Core Ops, SparseCore 0:
  52.0 21.2 all-gather.1
  91.1 14.2 reduce-scatter.1
where the time goes:
time: 114 us
  waiting for transfers between devices  47.8 us (42%)
  matrix products  28.6 us (25%)
  starting transfers between devices  15 us (13%)
  between operations  13.5 us (12%)
  other arithmetic  6.66 us (6%)
  local copies, waits for them, and re-layouts  2.15 us (2%)
    all_gather x1, waiting for transfers between devices, body(): gathered = lax.all_gather(attended, ('blk', 'rep'), axis=0, tiled=True)  21.4 us
    dot_general x1, matrix products, body(): jnp.dot(gathered, out_weight, preferred_element_type=jnp.float32)  17.6 us
    ppermute x12, starting transfers between devices, shifted(): lax.ppermute(x, axis, [(i, (i + by) % devices) for i in range(devices)])  15 us
    reduce_scatter x1, waiting for transfers between devices, body(): lax.psum_scatter(jnp.dot(gathered, out_weight, preferred_element_type=jnp...  14.4 us
    ppermute x12, waiting for transfers between devices, shifted(): lax.ppermute(x, axis, [(i, (i + by) % devices) for i in range(devices)])  12 us
    dot_general x4, matrix products, stop_partial(): jnp.einsum('rkgd,jkd->rkgj', queries, key_slot, preferred_element_type=jn...  6.03 us
    dot_general x4, matrix products, stop_partial(): jnp.einsum('rkgj,jkd->rkgd', weights.astype(jnp.bfloat16), value_slot, pr...  4.97 us
    reduce_sum x4, other arithmetic, stop_partial(): block_sum = jnp.sum(weights, axis=-1)  4.42 us
  transfers between devices with their start and end apart: 14, of which 7 were waited for; matrix products, arithmetic and copies ran while one was open for 12% of the time, Pallas kernels for 0%

commit v1 on v0

--- a/solution.py
+++ b/solution.py
@@ -4,6 +4,18 @@
 from jax.sharding import PartitionSpec as P
 
 NEG = -1e30
+
+
+def collect(x, axis, dim):
+    ways, here = (lax.axis_size(axis), lax.axis_index(axis))
+    grown, reach = (x, 1)
+    while reach < ways:
+        theirs = lax.ppermute(grown, axis, [(d, d ^ reach) for d in range(ways)])
+        mine_first = jnp.concatenate([grown, theirs], axis=dim)
+        theirs_first = jnp.concatenate([theirs, grown], axis=dim)
+        grown = jnp.where(here & reach == 0, mine_first, theirs_first)
+        reach = 2 * reach
+    return grown
 
 
 def shifted(x, axis, by):
@@ -75,7 +87,7 @@
     total_sum = jnp.sum(factors * jnp.stack(sums_home), axis=0)
     total_out = jnp.sum(factors[..., None] * jnp.stack(outs_home).astype(jnp.float32), axis=0)
     attended = (total_out / total_sum[..., None]).astype(jnp.bfloat16).reshape(row_count, -1)
-    gathered = lax.all_gather(attended, ("blk", "rep"), axis=0, tiled=True)
+    gathered = collect(attended, ("blk", "rep"), 0)
     projected = lax.psum_scatter(
         jnp.dot(gathered, out_weight, preferred_element_type=jnp.float32),
         "head",

time: 114 us -> 123 us (1.079)
  waiting for transfers between devices: 47.8 us -> 59.8 us
  matrix products: 28.6 us -> 25.4 us
    ppermute x0 -> x3, waiting for transfers between devices: none -> 33.9 us  [collect(): theirs = lax.ppermute(grown, axis, [(d, d ^ reach) for d in range(ways)])]
    all_gather x1 -> x0, waiting for transfers between devices: 21.4 us -> none  [body(): gathered = lax.all_gather(attended, ('blk', 'rep'), axis=0, tiled=True)]
    dot_general x1, matrix products: 17.6 us -> 14.4 us  [body(): jnp.dot(gathered, out_weight, preferred_element_type=jnp.float32)]
  transfers between devices with their start and end apart: 14 -> 16, of which waited for: 7 -> 9; matrix products, arithmetic and copies ran while one was open for 12% -> 11% of each run, Pallas kernels for 0% -> 0%
where the time goes in v1:
time: 123 us
  waiting for transfers between devices  59.8 us (49%)
  matrix products  25.4 us (21%)
  starting transfers between devices  16.2 us (13%)
  between operations  13.6 us (11%)
  other arithmetic  6.79 us (6%)
  local copies, waits for them, and re-layouts  1.49 us (1%)
    ppermute x3, waiting for transfers between devices, collect(): theirs = lax.ppermute(grown, axis, [(d, d ^ reach) for d in range(ways)])  33.9 us
    ppermute x12, starting transfers between devices, shifted(): lax.ppermute(x, axis, [(i, (i + by) % devices) for i in range(devices)])  15 us
    dot_general x1, matrix products, body(): jnp.dot(gathered, out_weight, preferred_element_type=jnp.float32)  14.4 us
    reduce_scatter x1, waiting for transfers between devices, body(): lax.psum_scatter(jnp.dot(gathered, out_weight, preferred_element_type=jnp...  13.8 us
    ppermute x12, waiting for transfers between devices, shifted(): lax.ppermute(x, axis, [(i, (i + by) % devices) for i in range(devices)])  12 us
    dot_general x4, matrix products, stop_partial(): jnp.einsum('rkgd,jkd->rkgj', queries, key_slot, preferred_element_type=jn...  6.03 us
    dot_general x4, matrix products, stop_partial(): jnp.einsum('rkgj,jkd->rkgd', weights.astype(jnp.bfloat16), value_slot, pr...  4.97 us
    reduce_sum x4, other arithmetic, stop_partial(): block_sum = jnp.sum(weights, axis=-1)  4.42 us
  transfers between devices with their start and end apart: 16, of which 9 were waited for; matrix products, arithmetic and copies ran while one was open for 11% of the time, Pallas kernels for 0%

profile of v1, /device:TPU:0, one launch (start us, length us, event | category | flops | bytes accessed | tf_op | source)
XLA Modules:
  0.0 123.2 jit_solution(1538564413968153774)
XLA Ops:
  6.5 3.1 %collective-permute-start = (bf16[8,8192]{1,0:T(8,128)(2,1)}, bf16[8,8192]{1,0:T(8,128)(2,1)S(1)}, u32[]{:S(2)}, u32[]{:S(2)}) collective-permute-start(bf16[8,8192]{1,0:T(8,128)(2,1)} %param.5), channel_id=1, source_target_pairs={{0,4},{4,8},{8,12},{12,0},{1,5},{5,9},{9,13},{13,1},{2,6},{6,10},{... | collective-permute-start | bytes 393224 | tf_op jit(solution)/shard_map/ppermute | solution.py:23
  9.6 0.9 fusion.119
  10.5 0.1 broadcast_compare_fusion.3
  10.6 2.7 %fusion.9 = (f32[8,4,16]{2,0,1:T(8,128)S(1)}, f32[4,2048,8,16]{1,3,2,0:T(8,128)S(1)}) fusion(pred[8,2048]{1,0:T(8,128)(4,1)S(1)} %get-tuple-element.7, bf16[8,4,16,128]{3,0,2,1:T(8,128)(2,1)} %bitcast.149, bf16[2048,4,128,1]{2,1,0,3:T(4,128)(2,1)} %bitcast.145), kind=kOutput, calls=%fused_computation.17 | convolution fusion | flops 271580672 | bytes 6440960 | tf_op jit(solution)/shard_map/rkgd,jkd->rkgj/dot_general | solution.py:32
  13.3 1.2 %fusion.91 = bf16[1,8,4,16,128]{4,3,1,2,0:T(8,128)(2,1)S(1)} fusion(bf16[2048,4,128,1]{2,1,0,3:T(4,128)(2,1)S(1)} %bitcast.121, f32[4,2048,8,16]{1,3,2,0:T(8,128)S(1)} %get-tuple-element.22, f32[8,4,16]{2,0,1:T(8,128)S(1)} %get-tuple-element.21, pred[8,2048]{1,0:T(8,128)(4,1)S(1)} %get-tuple-element.7), kind=kOutput, calls=%fused_computation.67 | convolution fusion | flops 272695296 | bytes 6440960 | tf_op jit(solution)/shard_map/rkgj,jkd->rkgd/dot_general | solution.py:39
  14.5 0.0 copy-start.1
  14.6 1.1 fusion.12
  15.7 0.4 copy-done.1
  16.1 1.1 fusion.6
  17.3 1.2 %fusion.86 = bf16[8,4,16,128]{3,2,0,1:T(8,128)(2,1)S(1)} fusion(bf16[2048,4,128,1]{2,1,0,3:T(4,128)(2,1)S(1)} %bitcast.124, f32[4,2048,8,16]{1,3,2,0:T(8,128)S(1)} %get-tuple-element.20, f32[8,4,16]{2,0,1:T(8,128)S(1)} %get-tuple-element.19, pred[8,2048]{1,0:T(8,128)(4,1)S(1)} %get-tuple-element.8), kind=kOutput, calls=%fused_computation.66 | convolution fusion | flops 272695296 | bytes 6440960 | tf_op jit(solution)/shard_map/rkgj,jkd->rkgd/dot_general | solution.py:39
  18.5 1.6 %collective-permute-start.2 = (bf16[8,8192]{1,0:T(8,128)(2,1)S(1)}, bf16[8,8192]{1,0:T(8,128)(2,1)S(1)}, u32[]{:S(2)}, u32[]{:S(2)}) collective-permute-start(bf16[8,8192]{1,0:T(8,128)(2,1)S(1)} %collective-permute-done), channel_id=1, source_target_pairs={{0,4},{4,8},{8,12},{12,0},{1,5},{5,9},{9,13},{13,1},{2,6},{6,10},{... | collective-permute-start | bytes 393224 | tf_op jit(solution)/shard_map/ppermute | solution.py:23
  20.1 1.1 fusion.14
  21.2 2.3 %collective-permute-start.1 = (f32[8,4,16]{2,0,1:T(8,128)S(1)}, f32[8,4,16]{2,0,1:T(8,128)S(1)}, u32[]{:S(2)}, u32[]{:S(2)}) collective-permute-start(f32[8,4,16]{2,0,1:T(8,128)S(1)} %get-tuple-element.19), channel_id=1, source_target_pairs={{0,12},{4,0},{8,4},{12,8},{1,13},{5,1},{9,5},{13,9},{2,14},{6,2},{... | collective-permute-start | bytes 6152 | tf_op jit(solution)/shard_map/ppermute | solution.py:23
  23.5 0.3 collective-permute-start.9
  23.8 2.0 %collective-permute-start.6 = (bf16[8,4,16,128]{3,2,0,1:T(8,128)(2,1)S(1)}, bf16[8,4,16,128]{3,2,0,1:T(8,128)(2,1)S(1)}, u32[]{:S(2)}, u32[]{:S(2)}) collective-permute-start(bf16[8,4,16,128]{3,2,0,1:T(8,128)(2,1)S(1)} %fusion.86), channel_id=1, source_target_pairs={{0,12},{4,0},{8,4},{12,8},{1,13},{5,1},{9,5},{13,9},{2,14},{6,2},{... | collective-permute-start | bytes 393224 | tf_op jit(solution)/shard_map/ppermute | solution.py:23
  25.8 0.0 collective-permute-done.2
  25.8 1.1 fusion.3
  26.9 1.2 %fusion.81 = bf16[8,4,16,128]{3,2,0,1:T(8,128)(2,1)S(1)} fusion(bf16[2048,4,128,1]{2,1,0,3:T(4,128)(2,1)S(1)} %bitcast.123, f32[4,2048,8,16]{1,3,2,0:T(8,128)S(1)} %get-tuple-element.18, f32[8,4,16]{2,0,1:T(8,128)S(1)} %get-tuple-element.17, pred[8,2048]{1,0:T(8,128)(4,1)S(1)} %get-tuple-element.9), kind=kOutput, calls=%fused_computation.65 | convolution fusion | flops 272695296 | bytes 6440960 | tf_op jit(solution)/shard_map/rkgj,jkd->rkgd/dot_general | solution.py:39
  28.2 0.3 collective-permute-start.4
  28.4 1.1 fusion.16
  29.5 1.2 collective-permute-start.3
  30.8 4.5 %collective-permute-done.4 = bf16[8,8192]{1,0:T(8,128)(2,1)S(1)} collective-permute-done((bf16[8,8192]{1,0:T(8,128)(2,1)S(1)}, bf16[8,8192]{1,0:T(8,128)(2,1)S(1)}, u32[]{:S(2)}, u32[]{:S(2)}) %collective-permute-start.4) | collective-permute-done | bytes 131104 | tf_op jit(solution)/shard_map/ppermute | solution.py:23
  35.3 1.1 fusion
  36.4 0.1 collective-permute-start.5
  36.5 1.2 %fusion.76 = bf16[8,4,16,128]{3,2,0,1:T(8,128)(2,1)S(1)} fusion(bf16[2048,4,128,1]{2,1,0,3:T(4,128)(2,1)S(1)} %bitcast.122, f32[4,2048,8,16]{1,3,2,0:T(8,128)S(1)} %get-tuple-element.16, f32[8,4,16]{2,0,1:T(8,128)S(1)} %get-tuple-element.15, pred[8,2048]{1,0:T(8,128)(4,1)S(1)} %get-tuple-element.10), kind=kOutput, calls=%fused_computation.64 | convolution fusion | flops 272695296 | bytes 6440960 | tf_op jit(solution)/shard_map/rkgj,jkd->rkgd/dot_general | solution.py:39
  37.7 1.1 fusion.18
  38.8 0.2 collective-permute-start.10
  39.0 2.8 %collective-permute-start.7 = (bf16[8,4,16,128]{3,2,0,1:T(8,128)(2,1)S(1)}, bf16[8,4,16,128]{3,2,0,1:T(8,128)(2,1)S(1)}, u32[]{:S(2)}, u32[]{:S(2)}) collective-permute-start(bf16[8,4,16,128]{3,2,0,1:T(8,128)(2,1)S(1)} %fusion.81), channel_id=1, source_target_pairs={{0,8},{4,12},{8,0},{12,4},{1,9},{5,13},{9,1},{13,5},{2,10},{6,14},... | collective-permute-start | bytes 393224 | tf_op jit(solution)/shard_map/ppermute | solution.py:23
  41.8 0.3 collective-permute-done.5
  42.1 1.2 collective-permute-start.11
  43.3 0.1 collective-permute-start.8
  43.4 2.8 %collective-permute-done.10 = f32[8,4,16]{2,0,1:T(8,128)S(1)} collective-permute-done((f32[8,4,16]{2,0,1:T(8,128)S(1)}, f32[8,4,16]{2,0,1:T(8,128)S(1)}, u32[]{:S(2)}, u32[]{:S(2)}) %collective-permute-start.10) | collective-permute-done | bytes 2080 | tf_op jit(solution)/shard_map/ppermute | solution.py:23
  46.2 2.6 %collective-permute-done.11 = f32[8,4,16]{2,0,1:T(8,128)S(1)} collective-permute-done((f32[8,4,16]{2,0,1:T(8,128)S(1)}, f32[8,4,16]{2,0,1:T(8,128)S(1)}, u32[]{:S(2)}, u32[]{:S(2)}) %collective-permute-start.11) | collective-permute-done | bytes 2080 | tf_op jit(solution)/shard_map/ppermute | solution.py:23
  48.9 1.7 %collective-permute-done.7 = bf16[8,4,16,128]{3,2,0,1:T(8,128)(2,1)S(1)} collective-permute-done((bf16[8,4,16,128]{3,2,0,1:T(8,128)(2,1)S(1)}, bf16[8,4,16,128]{3,2,0,1:T(8,128)(2,1)S(1)}, u32[]{:S(2)}, u32[]{:S(2)}) %collective-permute-start.7) | collective-permute-done | bytes 131104 | tf_op jit(solution)/shard_map/ppermute | solution.py:23
  50.6 0.3 multiply_reduce_fusion
  50.9 0.1 divide_convert_fusion
  51.1 0.1 copy.137
  51.2 0.1 collective-permute-start.12
  51.3 1.3 %collective-permute-done.12 = bf16[8,8192]{1,0:T(8,128)(2,1)S(1)} collective-permute-done((bf16[8,8192]{1,0:T(8,128)(2,1)S(1)}, bf16[8,8192]{1,0:T(8,128)(2,1)S(1)}, u32[]{:S(2)}, u32[]{:S(2)}) %collective-permute-start.12) | collective-permute-done | bytes 131104 | tf_op jit(solution)/shard_map/ppermute | solution.py:13
  52.7 0.1 collective-permute-start.13
  52.8 8.3 %collective-permute-done.13 = bf16[16,8192]{1,0:T(8,128)(2,1)S(1)} collective-permute-done((bf16[16,8192]{1,0:T(8,128)(2,1)S(1)}, bf16[16,8192]{1,0:T(8,128)(2,1)S(1)}, u32[]{:S(2)}, u32[]{:S(2)}) %collective-permute-start.13) | collective-permute-done | bytes 262176 | tf_op jit(solution)/shard_map/ppermute | solution.py:13
  61.1 0.1 maximum_select_fusion.2
  61.2 1.1 collective-permute-start.14
  62.3 24.3 %collective-permute-done.14 = bf16[32,8192]{1,0:T(8,128)(2,1)S(1)} collective-permute-done((bf16[32,8192]{1,0:T(8,128)(2,1)S(1)}, bf16[32,8192]{1,0:T(8,128)(2,1)S(1)}, u32[]{:S(2)}, u32[]{:S(2)}) %collective-permute-start.14) | collective-permute-done | bytes 524320 | tf_op jit(solution)/shard_map/ppermute | solution.py:13
  86.5 14.4 %fusion.96 = f32[64,2048]{1,0:T(8,128)} fusion(bf16[8192,2048]{1,0:T(8,128)(2,1)} %param.9, bf16[32,8192]{1,0:T(8,128)(2,1)S(1)} %collective-permute-done.14, bf16[32,8192]{1,0:T(8,128)(2,1)S(1)} %maximum_select_fusion.2, pred[]{:T(512)S(6)} %eq.14), kind=kOutput, calls=%fused_computation.69 | convolution fusion | flops 2152202240 | bytes 35127296 | tf_op jit(solution)/shard_map/dot_general | solution.py:92
  100.9 0.0 reduce-scatter.2.cloned.1.call-update
  100.9 13.8 %reduce-scatter.2.cloned.1.call-done = f32[32,2048]{1,0:T(8,128)} async-done(((f32[64,2048]{1,0:T(8,128)}), f32[32,2048]{1,0:T(8,128)}) %reduce-scatter.2.cloned.1.call-update) | async-done | bytes 262160 | tf_op jit(solution)/shard_map/reduce_scatter | solution.py:91
  114.7 1.6 %convert_element_type.64 = bf16[32,2048]{1,0:T(8,128)(2,1)} convert(f32[32,2048]{1,0:T(8,128)} %reduce-scatter.2.cloned.1.call-done) | non-fusion elementwise | flops 65536 | bytes 393216 | tf_op jit(solution)/shard_map/convert_element_type | solution.py:97
  (17 shorter events, 0.2 us)
Async XLA Ops:
  6.5 6.8 %copy-start = (bf16[1,1,2048,4,128]{4,3,2,1,0:T(4,128)(2,1)S(1)}, bf16[1,1,2048,4,128]{4,3,2,1,0:T(4,128)(2,1)}, u32[]{:S(2)}) copy-start(bf16[1,1,2048,4,128]{4,3,2,1,0:T(4,128)(2,1)} %param.7) | copy-start | bytes 6291460
  6.5 108.2 %reduce-scatter.2.cloned.1.call-start = ((), (), s32[]{:S(2)}) async-start(), calls=%async_computation.1 | async-start | bytes 786432 | tf_op jit(solution)/shard_map/reduce_scatter | solution.py:91
  6.5 9.1 %collective-permute-start = (bf16[8,8192]{1,0:T(8,128)(2,1)}, bf16[8,8192]{1,0:T(8,128)(2,1)S(1)}, u32[]{:S(2)}, u32[]{:S(2)}) collective-permute-start(bf16[8,8192]{1,0:T(8,128)(2,1)} %param.5), channel_id=1, source_target_pairs={{0,4},{4,8},{8,12},{12,0},{1,5},{5,9},{9,13},{13,1},{2,6},{6,10},{... | collective-permute-start | bytes 393224 | tf_op jit(solution)/shard_map/ppermute | solution.py:23
  14.5 1.6 %copy-start.1 = (bf16[1,1,2048,4,128]{4,3,2,1,0:T(4,128)(2,1)S(1)}, bf16[1,1,2048,4,128]{4,3,2,1,0:T(4,128)(2,1)}, u32[]{:S(2)}) copy-start(bf16[1,1,2048,4,128]{4,3,2,1,0:T(4,128)(2,1)} %param.6) | copy-start | bytes 6291460
  18.5 7.3 %collective-permute-start.2 = (bf16[8,8192]{1,0:T(8,128)(2,1)S(1)}, bf16[8,8192]{1,0:T(8,128)(2,1)S(1)}, u32[]{:S(2)}, u32[]{:S(2)}) collective-permute-start(bf16[8,8192]{1,0:T(8,128)(2,1)S(1)} %collective-permute-done), channel_id=1, source_target_pairs={{0,4},{4,8},{8,12},{12,0},{1,5},{5,9},{9,13},{13,1},{2,6},{6,10},{... | collective-permute-start | bytes 393224 | tf_op jit(solution)/shard_map/ppermute | solution.py:23
  21.2 17.6 %collective-permute-start.1 = (f32[8,4,16]{2,0,1:T(8,128)S(1)}, f32[8,4,16]{2,0,1:T(8,128)S(1)}, u32[]{:S(2)}, u32[]{:S(2)}) collective-permute-start(f32[8,4,16]{2,0,1:T(8,128)S(1)} %get-tuple-element.19), channel_id=1, source_target_pairs={{0,12},{4,0},{8,4},{12,8},{1,13},{5,1},{9,5},{13,9},{2,14},{6,2},{... | collective-permute-start | bytes 6152 | tf_op jit(solution)/shard_map/ppermute | solution.py:23
  23.5 19.8 %collective-permute-start.9 = (f32[8,4,16]{2,0,1:T(8,128)S(1)}, f32[8,4,16]{2,0,1:T(8,128)S(1)}, u32[]{:S(2)}, u32[]{:S(2)}) collective-permute-start(f32[8,4,16]{2,0,1:T(8,128)S(1)} %fusion.14), channel_id=1, source_target_pairs={{0,12},{4,0},{8,4},{12,8},{1,13},{5,1},{9,5},{13,9},{2,14},{6,2},{... | collective-permute-start | bytes 6152 | tf_op jit(solution)/shard_map/ppermute | solution.py:23
  23.8 25.0 %collective-permute-start.6 = (bf16[8,4,16,128]{3,2,0,1:T(8,128)(2,1)S(1)}, bf16[8,4,16,128]{3,2,0,1:T(8,128)(2,1)S(1)}, u32[]{:S(2)}, u32[]{:S(2)}) collective-permute-start(bf16[8,4,16,128]{3,2,0,1:T(8,128)(2,1)S(1)} %fusion.86), channel_id=1, source_target_pairs={{0,12},{4,0},{8,4},{12,8},{1,13},{5,1},{9,5},{13,9},{2,14},{6,2},{... | collective-permute-start | bytes 393224 | tf_op jit(solution)/shard_map/ppermute | solution.py:23
  28.2 7.1 %collective-permute-start.4 = (bf16[8,8192]{1,0:T(8,128)(2,1)S(1)}, bf16[8,8192]{1,0:T(8,128)(2,1)S(1)}, u32[]{:S(2)}, u32[]{:S(2)}) collective-permute-start(bf16[8,8192]{1,0:T(8,128)(2,1)S(1)} %collective-permute-done.2), channel_id=1, source_target_pairs={{0,4},{4,8},{8,12},{12,0},{1,5},{5,9},{9,13},{13,1},{2,6},{6,10},{... | collective-permute-start | bytes 393224 | tf_op jit(solution)/shard_map/ppermute | solution.py:23
  29.5 9.4 %collective-permute-start.3 = (f32[8,4,16]{2,0,1:T(8,128)S(1)}, f32[8,4,16]{2,0,1:T(8,128)S(1)}, u32[]{:S(2)}, u32[]{:S(2)}) collective-permute-start(f32[8,4,16]{2,0,1:T(8,128)S(1)} %get-tuple-element.17), channel_id=1, source_target_pairs={{0,8},{4,12},{8,0},{12,4},{1,9},{5,13},{9,1},{13,5},{2,10},{6,14},... | collective-permute-start | bytes 6152 | tf_op jit(solution)/shard_map/ppermute | solution.py:23
  36.4 5.7 %collective-permute-start.5 = (f32[8,4,16]{2,0,1:T(8,128)S(1)}, f32[8,4,16]{2,0,1:T(8,128)S(1)}, u32[]{:S(2)}, u32[]{:S(2)}) collective-permute-start(f32[8,4,16]{2,0,1:T(8,128)S(1)} %get-tuple-element.15), channel_id=1, source_target_pairs={{0,4},{4,8},{8,12},{12,0},{1,5},{5,9},{9,13},{13,1},{2,6},{6,10},{... | collective-permute-start | bytes 6152 | tf_op jit(solution)/shard_map/ppermute | solution.py:23
  38.8 7.4 %collective-permute-start.10 = (f32[8,4,16]{2,0,1:T(8,128)S(1)}, f32[8,4,16]{2,0,1:T(8,128)S(1)}, u32[]{:S(2)}, u32[]{:S(2)}) collective-permute-start(f32[8,4,16]{2,0,1:T(8,128)S(1)} %fusion.16), channel_id=1, source_target_pairs={{0,8},{4,12},{8,0},{12,4},{1,9},{5,13},{9,1},{13,5},{2,10},{6,14},... | collective-permute-start | bytes 6152 | tf_op jit(solution)/shard_map/ppermute | solution.py:23
  39.0 11.6 %collective-permute-start.7 = (bf16[8,4,16,128]{3,2,0,1:T(8,128)(2,1)S(1)}, bf16[8,4,16,128]{3,2,0,1:T(8,128)(2,1)S(1)}, u32[]{:S(2)}, u32[]{:S(2)}) collective-permute-start(bf16[8,4,16,128]{3,2,0,1:T(8,128)(2,1)S(1)} %fusion.81), channel_id=1, source_target_pairs={{0,8},{4,12},{8,0},{12,4},{1,9},{5,13},{9,1},{13,5},{2,10},{6,14},... | collective-permute-start | bytes 393224 | tf_op jit(solution)/shard_map/ppermute | solution.py:23
  42.1 6.7 %collective-permute-start.11 = (f32[8,4,16]{2,0,1:T(8,128)S(1)}, f32[8,4,16]{2,0,1:T(8,128)S(1)}, u32[]{:S(2)}, u32[]{:S(2)}) collective-permute-start(f32[8,4,16]{2,0,1:T(8,128)S(1)} %fusion.18), channel_id=1, source_target_pairs={{0,4},{4,8},{8,12},{12,0},{1,5},{5,9},{9,13},{13,1},{2,6},{6,10},{... | collective-permute-start | bytes 6152 | tf_op jit(solution)/shard_map/ppermute | solution.py:23
  43.3 7.3 %collective-permute-start.8 = (bf16[8,4,16,128]{3,2,0,1:T(8,128)(2,1)S(1)}, bf16[8,4,16,128]{3,2,0,1:T(8,128)(2,1)S(1)}, u32[]{:S(2)}, u32[]{:S(2)}) collective-permute-start(bf16[8,4,16,128]{3,2,0,1:T(8,128)(2,1)S(1)} %fusion.76), channel_id=1, source_target_pairs={{0,4},{4,8},{8,12},{12,0},{1,5},{5,9},{9,13},{13,1},{2,6},{6,10},{... | collective-permute-start | bytes 393224 | tf_op jit(solution)/shard_map/ppermute | solution.py:23
  51.2 1.4 %collective-permute-start.12 = (bf16[8,8192]{1,0:T(8,128)(2,1)S(1)}, bf16[8,8192]{1,0:T(8,128)(2,1)S(1)}, u32[]{:S(2)}, u32[]{:S(2)}) collective-permute-start(bf16[8,8192]{1,0:T(8,128)(2,1)S(1)} %bitcast.125), channel_id=1, source_target_pairs={{0,1},{1,0},{4,5},{5,4},{8,9},{9,8},{12,13},{13,12},{2,3},{3,2},{6... | collective-permute-start | bytes 393224 | tf_op jit(solution)/shard_map/ppermute | solution.py:13
  52.7 8.4 %collective-permute-start.13 = (bf16[16,8192]{1,0:T(8,128)(2,1)S(1)}, bf16[16,8192]{1,0:T(8,128)(2,1)S(1)}, u32[]{:S(2)}, u32[]{:S(2)}) collective-permute-start(bf16[16,8192]{1,0:T(8,128)(2,1)S(1)} %maximum_select_fusion.3), channel_id=1, source_target_pairs={{0,4},{1,5},{4,0},{5,1},{8,12},{9,13},{12,8},{13,9},{2,6},{3,7},{6... | collective-permute-start | bytes 786440 | tf_op jit(solution)/shard_map/ppermute | solution.py:13
  61.2 25.3 %collective-permute-start.14 = (bf16[32,8192]{1,0:T(8,128)(2,1)S(1)}, bf16[32,8192]{1,0:T(8,128)(2,1)S(1)}, u32[]{:S(2)}, u32[]{:S(2)}) collective-permute-start(bf16[32,8192]{1,0:T(8,128)(2,1)S(1)} %maximum_select_fusion.2), channel_id=1, source_target_pairs={{0,8},{1,9},{4,12},{5,13},{8,0},{9,1},{12,4},{13,5},{2,10},{3,11},... | collective-permute-start | bytes 1572872 | tf_op jit(solution)/shard_map/ppermute | solution.py:13
Sparse Core Ops, SparseCore 0:
  101.0 13.6 reduce-scatter.1
